TPU v7x, 128 devices: a whole 4x4x4 slice. The times are simulated.
128 devices in a mesh: expert: 16 (over y, x_lo, core), tensor: 8 (over x_hi, z).
Axes of the slice: x: 4 (x_hi: 2, x_lo: 2; x = x_hi * 2 + x_lo), y: 4, z: 4, core: 2. Of those that a mesh axis runs over, the one named last changes fastest.
Arguments:
- tokens: bfloat16 [4096, 7168], P(('expert', 'tensor')), may hold values from -6 to 6
- expert_ids: int32 [4096, 2], P('expert'), may hold values from 0 to 2, all different within a row
- gate_scores: int32 [4096, 2], P('expert'), may hold values from 1 to 64
- gate_weight: bfloat16 [3, 7168, 2048], P(None, ('expert', 'tensor')), may hold values from -0.0625 to 0.0625
- up_weight: bfloat16 [3, 7168, 2048], P(None, ('expert', 'tensor')), may hold values from -0.0625 to 0.0625
- down_weight: bfloat16 [3, 7168, 2048], P(None, ('expert', 'tensor')), may hold values from -0.1875 to 0.1875
Outputs:
- mixed: bfloat16 [4096, 7168], P(('expert', 'tensor'))
Inputs may be any that keep to these rules, and one draw needn't show every extreme that they name: `expert_ids`: each row names 2 different experts.
All inputs are finite; a program needn't handle non-finite values.
Results may differ from a plain program's by a relative error of at most 0.015.
Values may be sent and summed in bfloat16 or wider, within the bound.
A program may use at most 128 MiB of HBM per device.

v0:
```python
import jax
import jax.numpy as jnp
from jax import lax
from jax.sharding import PartitionSpec as P


def activate(gate_sum, up_sum, weight_col):
    return (jax.nn.silu(gate_sum) * up_sum * weight_col).astype(jnp.bfloat16)


def local(tokens, expert_ids, gate_scores, gate_weight, up_weight, down_weight):
    gathered = lax.all_gather(tokens, "tensor", axis=0, tiled=True)
    experts = gate_weight.shape[0]
    scores = gate_scores.astype(jnp.float32)
    score_sum = jnp.sum(scores, axis=1, keepdims=True)
    labels = jnp.arange(experts, dtype=jnp.int32)
    picked = (expert_ids[:, :, None] == labels[None, None, :]).astype(jnp.float32)
    combine = jnp.sum(scores[:, :, None] * picked, axis=1) / score_sum
    served_gate, served_up, served_down = (
        lax.all_to_all(gate_weight, "tensor", split_axis=2, concat_axis=1, tiled=True),
        lax.all_to_all(up_weight, "tensor", split_axis=2, concat_axis=1, tiled=True),
        lax.all_to_all(down_weight, "tensor", split_axis=2, concat_axis=1, tiled=True),
    )
    hiddens = []
    full_gate, full_up = (
        lax.all_gather(served_gate, "expert", axis=1, tiled=True),
        lax.all_gather(served_up, "expert", axis=1, tiled=True),
    )
    for which in range(experts):
        gate_sum = jnp.dot(gathered, full_gate[which], preferred_element_type=jnp.float32)
        up_sum = jnp.dot(gathered, full_up[which], preferred_element_type=jnp.float32)
        hiddens.append(activate(gate_sum, up_sum, combine[:, which : which + 1]))
    stacked = jnp.stack(hiddens)
    partial_sum = jnp.einsum(
        "etf,edf->td",
        stacked,
        lax.all_gather(served_down, "expert", axis=1, tiled=True),
        preferred_element_type=jnp.float32,
    )
    output_rows = lax.psum_scatter(
        partial_sum.astype(jnp.bfloat16), "tensor", scatter_dimension=0, tiled=True
    )
    return output_rows


def solution(mesh):
    return jax.shard_map(
        local,
        mesh=mesh,
        in_specs=(
            P(("expert", "tensor"), None),
            P("expert", None),
            P("expert", None),
            P(None, ("expert", "tensor"), None),
            P(None, ("expert", "tensor"), None),
            P(None, ("expert", "tensor"), None),
        ),
        out_specs=P(("expert", "tensor"), None),
        check_vma=False,
    )
```

profile of v0, /device:TPU:0, one launch (start us, length us, event | category | flops | bytes accessed | tf_op | source)
XLA Modules:
  0.0 393.2 jit_solution(62899333029683740)
XLA Ops:
  6.5 0.0 all-gather.5.cloned.1.call-start
  6.5 0.7 all-gather.5.cloned.1.call-update
  7.3 0.0 all-gather.7.cloned.1.call-start
  7.3 2.8 copy.28
  10.1 2.7 reshape.8
  12.8 25.9 %all_to_all.54 = bf16[8,2,21504]{2,1,0:T(2,128)(2,1)S(1)} all-to-all(bf16[8,2,21504]{2,1,0:T(2,128)(2,1)S(1)} %reshape.8), channel_id=1, replica_groups=mesh['expert'=16,'tensor'=8] {'tensor'}, dimensions={0} | all-to-all | bytes 1376256 | tf_op jit(solution)/shard_map/all_to_all | solution.py:20
  38.8 0.0 copy-start
  38.8 3.0 reshape.9
  41.8 2.1 copy.37
  43.9 0.0 all-gather.7.cloned.1.call-update
  44.0 0.0 all-gather.9.cloned.1.call-start
  44.0 0.0 copy-done
  44.0 1.4 copy.31
  45.4 2.7 reshape.6
  48.1 20.4 %all_to_all.55 = bf16[8,2,21504]{2,1,0:T(2,128)(2,1)S(1)} all-to-all(bf16[8,2,21504]{2,1,0:T(2,128)(2,1)S(1)} %reshape.6), channel_id=1, replica_groups=mesh['expert'=16,'tensor'=8] {'tensor'}, dimensions={0} | all-to-all | bytes 1376256 | tf_op jit(solution)/shard_map/all_to_all | solution.py:21
  68.5 0.0 copy-start.1
  68.5 3.0 reshape.7
  71.5 2.2 copy.39
  73.7 0.0 all-gather.9.cloned.1.call-update
  73.7 0.0 all-gather.11.cloned.1.call-start
  73.8 0.0 copy-done.1
  73.8 1.4 copy.34
  75.1 2.7 reshape.4
  77.8 0.0 copy-start.2
  77.9 0.0 copy-start.3
  77.9 14.4 %all_to_all.56 = bf16[8,2,21504]{2,1,0:T(2,128)(2,1)S(1)} all-to-all(bf16[8,2,21504]{2,1,0:T(2,128)(2,1)S(1)} %reshape.4), channel_id=1, replica_groups=mesh['expert'=16,'tensor'=8] {'tensor'}, dimensions={0} | all-to-all | bytes 1376256 | tf_op jit(solution)/shard_map/all_to_all | solution.py:22
  92.2 3.0 reshape.5
  95.2 2.2 copy.35
  97.4 0.0 all-gather.11.cloned.1.call-update
  97.4 0.2 reduce-scatter.2.cloned.1.call-start
  97.6 0.0 copy-done.2
  97.7 0.0 copy-done.3
  97.7 0.0 all-gather.5.cloned.1.call-done
  97.8 58.9 %all-gather.7.cloned.1.call-done = bf16[3,7168,256]{2,1,0:T(8,128)(2,1)} async-done(((bf16[3,448,256]{2,1,0:T(8,128)(2,1)}), bf16[3,7168,256]{2,1,0:T(8,128)(2,1)}) %all-gather.7.cloned.1.call-update) | async-done | bytes 11010064 | tf_op jit(solution)/shard_map/all_gather | solution.py:26
  156.7 0.0 copy-start.4
  156.7 4.4 %fusion.2 = f32[256,256]{1,0:T(8,128)S(1)} fusion(bf16[256,7168]{1,0:T(8,128)(2,1)} %all-gather.5.cloned.1.call-done, bf16[3,7168,256]{2,1,0:T(8,128)(2,1)} %all-gather.7.cloned.1.call-done), kind=kOutput, calls=%fused_computation.5 | convolution fusion | flops 939524096 | bytes 7602176 | tf_op jit(solution)/shard_map/dot_general | solution.py:30
  161.1 0.0 copy-done.4
  161.1 3.2 fusion.4
  164.3 3.2 fusion.6
  167.6 56.2 %all-gather.9.cloned.1.call-done = bf16[3,7168,256]{2,1,0:T(8,128)(2,1)} async-done(((bf16[3,448,256]{2,1,0:T(8,128)(2,1)}), bf16[3,7168,256]{2,1,0:T(8,128)(2,1)}) %all-gather.9.cloned.1.call-update) | async-done | bytes 11010064 | tf_op jit(solution)/shard_map/all_gather | solution.py:27
  223.8 4.4 %fusion.18 = bf16[1,256,256]{2,1,0:T(8,128)(2,1)S(1)} fusion(bf16[256,7168]{1,0:T(8,128)(2,1)} %all-gather.5.cloned.1.call-done, bf16[3,7168,256]{2,1,0:T(8,128)(2,1)} %all-gather.9.cloned.1.call-done, f32[256,256]{1,0:T(8,128)S(1)} %fusion.2, f32[256]{0:T(256)S(1)} %bitcast.93), kind=kOutput, calls=%fused_computation.25 | convolution fusion | flops 939982848 | bytes 7734272 | tf_op jit(solution)/shard_map/dot_general | solution.py:31
  228.2 0.0 copy-done.5
  228.2 3.2 fusion.17
  231.4 3.2 fusion.16
  234.6 56.2 %all-gather.11.cloned.1.call-done = bf16[3,7168,256]{2,1,0:T(8,128)(2,1)} async-done(((bf16[3,448,256]{2,1,0:T(8,128)(2,1)}), bf16[3,7168,256]{2,1,0:T(8,128)(2,1)}) %all-gather.11.cloned.1.call-update) | async-done | bytes 11010064 | tf_op jit(solution)/shard_map/all_gather | solution.py:37
  290.8 12.7 %fusion = bf16[256,7168]{1,0:T(8,128)(2,1)} fusion(bf16[3,7168,256]{2,1,0:T(8,128)(2,1)} %all-gather.11.cloned.1.call-done, bf16[1,256,256]{2,1,0:T(8,128)(2,1)S(1)} %fusion.18, bf16[1,256,256]{2,1,0:T(8,128)(2,1)S(1)} %fusion.17, bf16[1,256,256]{2,1,0:T(8,128)(2,1)S(1)} %fusion.16), kind=kOutput, calls=%fused_computation.1 | convolution fusion | flops 2820800512 | bytes 15073280 | tf_op jit(solution)/shard_map/etf,edf->td/dot_general | solution.py:34
  303.4 0.0 reduce-scatter.2.cloned.1.call-update
  303.5 83.2 %reduce-scatter.2.cloned.1.call-done = bf16[32,7168]{1,0:T(8,128)(2,1)} async-done(((bf16[256,7168]{1,0:T(8,128)(2,1)}), bf16[32,7168]{1,0:T(8,128)(2,1)}) %reduce-scatter.2.cloned.1.call-update) | async-done | bytes 458768 | tf_op jit(solution)/shard_map/reduce_scatter | solution.py:40
  (6 shorter events, 0.1 us)
Async XLA Ops:
  6.5 91.2 %all-gather.5.cloned.1.call-start = ((), (), s32[]{:S(2)}) async-start(), calls=%async_computation.4 | async-start | bytes 4128768 | tf_op jit(solution)/shard_map/all_gather | solution.py:12
  7.3 149.4 %all-gather.7.cloned.1.call-start = ((), (), s32[]{:S(2)}) async-start(), calls=%async_computation.5 | async-start | bytes 11698176 | tf_op jit(solution)/shard_map/all_gather | solution.py:26
  38.8 5.2 %copy-start = (bf16[3,56,2048]{2,1,0:T(8,128)(2,1)S(1)}, bf16[3,56,2048]{2,1,0:T(8,128)(2,1)}, u32[]{:S(2)}) copy-start(bf16[3,56,2048]{2,1,0:T(8,128)(2,1)} %param.10) | copy-start | bytes 2064388
  44.0 179.8 %all-gather.9.cloned.1.call-start = ((), (), s32[]{:S(2)}) async-start(), calls=%async_computation.6 | async-start | bytes 11698176 | tf_op jit(solution)/shard_map/all_gather | solution.py:27
  68.5 5.3 %copy-start.1 = (bf16[3,56,2048]{2,1,0:T(8,128)(2,1)S(1)}, bf16[3,56,2048]{2,1,0:T(8,128)(2,1)}, u32[]{:S(2)}) copy-start(bf16[3,56,2048]{2,1,0:T(8,128)(2,1)} %param.11) | copy-start | bytes 2064388
  73.7 217.1 %all-gather.11.cloned.1.call-start = ((), (), s32[]{:S(2)}) async-start(), calls=%async_computation.7 | async-start | bytes 11698176 | tf_op jit(solution)/shard_map/all_gather | solution.py:37
  77.8 19.8 %copy-start.2 = (s32[256,2]{0,1:T(2,128)S(1)}, s32[256,2]{0,1:T(2,128)}, u32[]{:S(2)}) copy-start(s32[256,2]{0,1:T(2,128)} %param.8) | copy-start | bytes 6148
  77.9 19.8 %copy-start.3 = (s32[256,2]{0,1:T(2,128)S(1)}, s32[256,2]{0,1:T(2,128)}, u32[]{:S(2)}) copy-start(s32[256,2]{0,1:T(2,128)} %param.7) | copy-start | bytes 6148
  97.4 289.3 %reduce-scatter.2.cloned.1.call-start = ((), (), s32[]{:S(2)}) async-start(), calls=%async_computation.8 | async-start | bytes 4128768 | tf_op jit(solution)/shard_map/reduce_scatter | solution.py:40
  156.7 4.4 %copy-start.4 = (bf16[256,7168]{1,0:T(8,128)(2,1)S(1)}, bf16[256,7168]{1,0:T(8,128)(2,1)}, u32[]{:S(2)}) copy-start(bf16[256,7168]{1,0:T(8,128)(2,1)} %all-gather.5.cloned.1.call-done) | copy-start | bytes 11010052
  223.8 4.4 %copy-start.5 = (bf16[256,7168]{1,0:T(8,128)(2,1)S(1)}, bf16[256,7168]{1,0:T(8,128)(2,1)}, u32[]{:S(2)}) copy-start(bf16[256,7168]{1,0:T(8,128)(2,1)} %all-gather.5.cloned.1.call-done) | copy-start | bytes 11010052
Sparse Core Ops, SparseCore 0:
  9.7 83.9 all-gather.4
  95.3 61.3 all-gather.6
  158.4 65.3 all-gather.8
  225.3 65.3 all-gather.10
  303.6 83.0 reduce-scatter.1
where the time goes:
time: 394 us; the launch traced here: 393 us
  waiting for transfers between devices  255 us (65%)
  blocking collectives  60.7 us (15%)
  matrix products  34.3 us (9%)
  local copies, waits for them, and re-layouts  29.2 us (7%)
  between operations  13.3 us (3%)
    reduce_scatter x1, waiting for transfers between devices, local(): lax.psum_scatter(partial_sum.astype(jnp.bfloat16), 'tensor', scatter_dime...  83.2 us
    all_gather x1, waiting for transfers between devices, local(): lax.all_gather(served_gate, 'expert', axis=1, tiled=True)  58.9 us
    all_gather x1, waiting for transfers between devices, local(): lax.all_gather(served_up, 'expert', axis=1, tiled=True)  56.2 us
    all_gather x1, waiting for transfers between devices, local(): lax.all_gather(served_down, 'expert', axis=1, tiled=True)  56.2 us
    all_to_all x1, blocking collectives, local(): lax.all_to_all(gate_weight, 'tensor', split_axis=2, concat_axis=1, tiled=...  25.9 us
    unnamed x21, local copies, waits for them, and re-layouts  22.7 us
    all_to_all x1, blocking collectives, local(): lax.all_to_all(up_weight, 'tensor', split_axis=2, concat_axis=1, tiled=True)  20.4 us
    all_to_all x1, blocking collectives, local(): lax.all_to_all(down_weight, 'tensor', split_axis=2, concat_axis=1, tiled=...  14.4 us
  transfers between devices with their start and end apart: 5, of which 4 were waited for; matrix products, arithmetic and copies ran while one was open for 13% of the time, Pallas kernels for 0%

commit v1 on v0

--- a/solution.py
+++ b/solution.py
@@ -2,6 +2,7 @@
 import jax.numpy as jnp
 from jax import lax
 from jax.sharding import PartitionSpec as P
+from jax.lax import all_to_all, axis_size
 
 
 def activate(gate_sum, up_sum, weight_col):
@@ -9,6 +10,13 @@
 
 
 def local(tokens, expert_ids, gate_scores, gate_weight, up_weight, down_weight):
+
+    def make_records(original, comm_axis, out_dim):
+        return jnp.concatenate(
+            all_to_all(jnp.stack(axis_size(comm_axis) * [original], axis=0), comm_axis, 0, 0),
+            out_dim,
+        )
+
     gathered = lax.all_gather(tokens, "tensor", axis=0, tiled=True)
     experts = gate_weight.shape[0]
     scores = gate_scores.astype(jnp.float32)
@@ -24,7 +32,7 @@
     hiddens = []
     full_gate, full_up = (
         lax.all_gather(served_gate, "expert", axis=1, tiled=True),
-        lax.all_gather(served_up, "expert", axis=1, tiled=True),
+        make_records(served_up, "expert", 1),
     )
     for which in range(experts):
         gate_sum = jnp.dot(gathered, full_gate[which], preferred_element_type=jnp.float32)

time: 394 us -> 459 us (1.16)
  waiting for transfers between devices: 255 us -> 308 us
  local copies, waits for them, and re-layouts: 29.2 us -> 45 us
  matrix products: 34.3 us -> 25.7 us
  starting transfers between devices: 0.35 us -> 5.7 us
    all_to_all x0 -> x1, waiting for transfers between devices: none -> 189 us  [make_records(): all_to_all(jnp.stack(axis_size(comm_axis) * [original], axis=0), comm_axi...]
    all_gather x1, waiting for transfers between devices: 58.9 us -> 0.01 us  [local(): lax.all_gather(served_gate, 'expert', axis=1, tiled=True)]
    all_gather x1 -> x0, waiting for transfers between devices: 56.2 us -> none  [local(): lax.all_gather(served_up, 'expert', axis=1, tiled=True)]
    all_gather x1, waiting for transfers between devices: 56.2 us -> 35 us  [local(): lax.all_gather(served_down, 'expert', axis=1, tiled=True)]
    slice x0 -> x1, local copies, waits for them, and re-layouts: none -> 7.94 us  [local(): full_up[which]]
    all_to_all x1, blocking collectives: 14.4 us -> 20.4 us  [local(): lax.all_to_all(down_weight, 'tensor', split_axis=2, concat_axis=1, tiled=...]
    all_to_all x1, blocking collectives: 20.4 us -> 14.3 us  [local(): lax.all_to_all(up_weight, 'tensor', split_axis=2, concat_axis=1, tiled=True)]
    another operation x0 -> x1, local copies, waits for them, and re-layouts: none -> 5.43 us  [make_records(): jnp.stack(axis_size(comm_axis) * [original], axis=0)]
  transfers between devices with their start and end apart: 5 -> 5, of which waited for: 4 -> 3; matrix products, arithmetic and copies ran while one was open for 13% -> 12% of each run, Pallas kernels for 0% -> 0%
where the time goes in v1:
time: 459 us
  waiting for transfers between devices  308 us (67%)
  blocking collectives  60.7 us (13%)
  local copies, waits for them, and re-layouts  45 us (10%)
  matrix products  25.7 us (6%)
  between operations  13.4 us (3%)
  starting transfers between devices  5.7 us (1%)
    all_to_all x1, waiting for transfers between devices, make_records(): all_to_all(jnp.stack(axis_size(comm_axis) * [original], axis=0), comm_axi...  189 us
    reduce_scatter x1, waiting for transfers between devices, local(): lax.psum_scatter(partial_sum.astype(jnp.bfloat16), 'tensor', scatter_dime...  83.5 us
    all_gather x1, waiting for transfers between devices, local(): lax.all_gather(served_down, 'expert', axis=1, tiled=True)  35 us
    unnamed x27, local copies, waits for them, and re-layouts  26.2 us
    all_to_all x1, blocking collectives, local(): lax.all_to_all(gate_weight, 'tensor', split_axis=2, concat_axis=1, tiled=...  25.9 us
    all_to_all x1, blocking collectives, local(): lax.all_to_all(down_weight, 'tensor', split_axis=2, concat_axis=1, tiled=...  20.4 us
    all_to_all x1, blocking collectives, local(): lax.all_to_all(up_weight, 'tensor', split_axis=2, concat_axis=1, tiled=True)  14.3 us
    dot_general x1, matrix products, local(): jnp.einsum('etf,edf->td', stacked, lax.all_gather(served_down, 'expert',...  12.5 us
  transfers between devices with their start and end apart: 5, of which 3 were waited for; matrix products, arithmetic and copies ran while one was open for 12% of the time, Pallas kernels for 0%

profile of v1, /device:TPU:0, one launch (start us, length us, event | category | flops | bytes accessed | tf_op | source)
XLA Modules:
  0.0 458.5 jit_solution(9005072131616238800)
XLA Ops:
  6.5 0.0 all-gather.4.cloned.1.call-start
  6.5 0.7 all-gather.4.cloned.1.call-update
  7.3 0.0 all-gather.6.cloned.1.call-start
  7.3 2.8 copy.28
  10.1 2.7 reshape.22
  12.8 25.9 %all_to_all.56 = bf16[8,2,21504]{2,1,0:T(2,128)(2,1)S(1)} all-to-all(bf16[8,2,21504]{2,1,0:T(2,128)(2,1)S(1)} %reshape.22), channel_id=1, replica_groups=mesh['expert'=16,'tensor'=8] {'tensor'}, dimensions={0} | all-to-all | bytes 1376256 | tf_op jit(solution)/shard_map/all_to_all | solution.py:28
  38.8 3.0 reshape.23
  41.8 2.2 copy.37
  44.0 0.0 all-gather.6.cloned.1.call-update
  44.0 0.0 all-gather.8.cloned.1.call-start
  44.0 0.0 copy-done.3
  44.0 1.4 copy.34
  45.4 2.7 reshape.18
  48.1 20.4 %all_to_all.57 = bf16[8,2,21504]{2,1,0:T(2,128)(2,1)S(1)} all-to-all(bf16[8,2,21504]{2,1,0:T(2,128)(2,1)S(1)} %reshape.18), channel_id=1, replica_groups=mesh['expert'=16,'tensor'=8] {'tensor'}, dimensions={0} | all-to-all | bytes 1376256 | tf_op jit(solution)/shard_map/all_to_all | solution.py:30
  68.5 3.0 reshape.19
  71.5 2.2 copy.35
  73.7 0.0 all-gather.8.cloned.1.call-update
  73.7 0.0 copy-done.4
  73.8 1.4 copy.31
  75.1 2.7 reshape.20
  77.8 14.3 %all_to_all.58 = bf16[8,2,21504]{2,1,0:T(2,128)(2,1)S(1)} all-to-all(bf16[8,2,21504]{2,1,0:T(2,128)(2,1)S(1)} %reshape.20), channel_id=1, replica_groups=mesh['expert'=16,'tensor'=8] {'tensor'}, dimensions={0} | all-to-all | bytes 1376256 | tf_op jit(solution)/shard_map/all_to_all | solution.py:29
  92.2 3.0 reshape.21
  95.2 1.1 copy.39
  96.3 5.4 %stack.13 = bf16[16,3,448,256]{3,2,1,0:T(8,128)(2,1)} broadcast(bf16[3,448,256]{2,1,0:T(8,128)(2,1)S(1)} %bitcast.67), dimensions={1,2,3} | broadcast | bytes 11698176 | tf_op jit(solution)/shard_map/stack | solution.py:16
  101.7 5.4 %all-to-all-start.2 = ((bf16[16,3,448,256]{3,2,1,0:T(8,128)(2,1)}), bf16[16,3,448,256]{3,2,1,0:T(8,128)(2,1)}, u32[]{:S(2)}, u32[]{:S(2)}) async-start(bf16[16,3,448,256]{3,2,1,0:T(8,128)(2,1)} %stack.13), calls=%async_computation.2 | async-start | bytes 22020096 | tf_op jit(solution)/shard_map/all_to_all | solution.py:16
  107.1 0.2 reduce-scatter.2.cloned.1.call-start
  107.4 0.0 copy-done.5
  107.4 0.0 copy-done.6
  107.4 188.8 %all-to-all-done.2 = bf16[16,3,448,256]{3,2,1,0:T(8,128)(2,1)} async-done(((bf16[16,3,448,256]{3,2,1,0:T(8,128)(2,1)}), bf16[16,3,448,256]{3,2,1,0:T(8,128)(2,1)}, u32[]{:S(2)}, u32[]{:S(2)}) %all-to-all-start.2) | async-done | bytes 11010080 | tf_op jit(solution)/shard_map/all_to_all | solution.py:16
  296.2 7.9 %fusion.20 = (bf16[1,16,448,256]{3,2,0,1:T(8,128)(2,1)}, bf16[1,16,448,256]{3,2,0,1:T(8,128)(2,1)}, bf16[1,16,448,256]{3,2,0,1:T(8,128)(2,1)}) fusion(bf16[3,16,448,256]{3,2,0,1:T(8,128)(2,1)} %bitcast.9), kind=kLoop, calls=%fused_computation.30 | loop fusion | bytes 22020096 | tf_op jit(solution)/shard_map/slice | solution.py:39
  304.2 0.0 copy-start.7
  304.2 4.5 fusion.1
  308.7 0.0 copy-done.2
  308.7 0.0 copy-start.8
  308.7 4.2 fusion.10
  312.9 0.2 copy-done.7
  313.1 1.4 copy-done.8
  314.5 1.1 fusion.2
  315.6 1.0 copy-done.1
  316.6 1.1 fusion.11
  317.7 0.0 copy-start
  317.7 1.1 fusion.3
  318.8 1.0 copy-done
  319.8 1.1 fusion.12
  321.0 35.0 %all-gather.8.cloned.1.call-done = bf16[3,7168,256]{2,1,0:T(8,128)(2,1)} async-done(((bf16[3,448,256]{2,1,0:T(8,128)(2,1)}), bf16[3,7168,256]{2,1,0:T(8,128)(2,1)}) %all-gather.8.cloned.1.call-update) | async-done | bytes 11010064 | tf_op jit(solution)/shard_map/all_gather | solution.py:45
  356.0 12.5 %fusion = bf16[256,7168]{1,0:T(8,128)(2,1)} fusion(bf16[3,7168,256]{2,1,0:T(8,128)(2,1)} %all-gather.8.cloned.1.call-done, bf16[1,256,256]{2,1,0:T(8,128)(2,1)S(1)} %fusion.10, bf16[1,256,256]{2,1,0:T(8,128)(2,1)S(1)} %fusion.11, bf16[1,256,256]{2,1,0:T(8,128)(2,1)S(1)} %fusion.12), kind=kOutput, calls=%fused_computation.1 | convolution fusion | flops 2820800512 | bytes 15073280 | tf_op jit(solution)/shard_map/etf,edf->td/dot_general | solution.py:42
  368.5 0.0 reduce-scatter.2.cloned.1.call-update
  368.5 83.5 %reduce-scatter.2.cloned.1.call-done = bf16[32,7168]{1,0:T(8,128)(2,1)} async-done(((bf16[256,7168]{1,0:T(8,128)(2,1)}), bf16[32,7168]{1,0:T(8,128)(2,1)}) %reduce-scatter.2.cloned.1.call-update) | async-done | bytes 458768 | tf_op jit(solution)/shard_map/reduce_scatter | solution.py:48
  (13 shorter events, 0.1 us)
Async XLA Ops:
  6.5 297.6 %all-gather.4.cloned.1.call-start = ((), (), s32[]{:S(2)}) async-start(), calls=%async_computation.5 | async-start | bytes 4128768 | tf_op jit(solution)/shard_map/all_gather | solution.py:20
  7.3 296.9 %all-gather.6.cloned.1.call-start = ((), (), s32[]{:S(2)}) async-start(), calls=%async_computation.6 | async-start | bytes 11698176 | tf_op jit(solution)/shard_map/all_gather | solution.py:34
  38.8 5.3 %copy-start.3 = (bf16[3,56,2048]{2,1,0:T(8,128)(2,1)S(1)}, bf16[3,56,2048]{2,1,0:T(8,128)(2,1)}, u32[]{:S(2)}) copy-start(bf16[3,56,2048]{2,1,0:T(8,128)(2,1)} %param.11) | copy-start | bytes 2064388
  44.0 312.0 %all-gather.8.cloned.1.call-start = ((), (), s32[]{:S(2)}) async-start(), calls=%async_computation.7 | async-start | bytes 11698176 | tf_op jit(solution)/shard_map/all_gather | solution.py:45
  68.5 5.2 %copy-start.4 = (bf16[3,56,2048]{2,1,0:T(8,128)(2,1)S(1)}, bf16[3,56,2048]{2,1,0:T(8,128)(2,1)}, u32[]{:S(2)}) copy-start(bf16[3,56,2048]{2,1,0:T(8,128)(2,1)} %param.10) | copy-start | bytes 2064388
  101.7 5.6 %copy-start.5 = (s32[256,2]{0,1:T(2,128)S(1)}, s32[256,2]{0,1:T(2,128)}, u32[]{:S(2)}) copy-start(s32[256,2]{0,1:T(2,128)} %param.8) | copy-start | bytes 6148
  101.7 5.7 %copy-start.6 = (s32[256,2]{0,1:T(2,128)S(1)}, s32[256,2]{0,1:T(2,128)}, u32[]{:S(2)}) copy-start(s32[256,2]{0,1:T(2,128)} %param.7) | copy-start | bytes 6148
  101.7 194.5 %all-to-all-start.2 = ((bf16[16,3,448,256]{3,2,1,0:T(8,128)(2,1)}), bf16[16,3,448,256]{3,2,1,0:T(8,128)(2,1)}, u32[]{:S(2)}, u32[]{:S(2)}) async-start(bf16[16,3,448,256]{3,2,1,0:T(8,128)(2,1)} %stack.13), calls=%async_computation.2 | async-start | bytes 22020096 | tf_op jit(solution)/shard_map/all_to_all | solution.py:16
  107.1 344.9 %reduce-scatter.2.cloned.1.call-start = ((), (), s32[]{:S(2)}) async-start(), calls=%async_computation.8 | async-start | bytes 4128768 | tf_op jit(solution)/shard_map/reduce_scatter | solution.py:48
  304.2 4.5 copy-start.2
  304.2 9.0 %copy-start.7 = (bf16[3,7168,256]{2,1,0:T(8,128)(2,1)S(1)}, bf16[3,7168,256]{2,1,0:T(8,128)(2,1)}, u32[]{:S(2)}) copy-start(bf16[3,7168,256]{2,1,0:T(8,128)(2,1)} %all-gather.6.cloned.1.call-done) | copy-start | bytes 33030148
  308.7 5.8 %copy-start.8 = (bf16[256,7168]{1,0:T(8,128)(2,1)S(1)}, bf16[256,7168]{1,0:T(8,128)(2,1)}, u32[]{:S(2)}) copy-start(bf16[256,7168]{1,0:T(8,128)(2,1)} %all-gather.4.cloned.1.call-done) | copy-start | bytes 11010052
  314.5 2.1 copy-start.1
  317.7 2.2 copy-start
Sparse Core Ops, SparseCore 0:
  9.7 83.9 all-gather.3
  95.3 185.5 all-gather.5
  282.6 73.3 all-gather.7
  368.6 83.3 reduce-scatter.1
